TPU v7x, 32 devices: a whole 2x2x4 slice. The times are simulated.
32 devices in a mesh: grp: 4 (over y, core), mem: 8 (over z, x).
Axes of the slice: x: 2, y: 2, z: 4, core: 2. Of those that a mesh axis runs over, the one named last changes fastest.
Arguments:
- video: bfloat16 [32, 32, 32, 1024], P('mem', 'grp'), may hold values from -6 to 6
- w_triple: bfloat16 [2, 1024, 3072], replicated, may hold values from -0.75 to 0.75, as said below
- w_out: bfloat16 [2, 1024, 1024], replicated, may hold values from -0.1875 to 0.1875
Outputs:
- result: bfloat16 [32, 32, 32, 1024], P('mem', 'grp')
Inputs may be any that keep to these rules, and one draw needn't show every extreme that they name: `w_triple`: entries of order 1024 ** -0.5, independent between columns of values.
All inputs are finite; a program needn't handle non-finite values.
Results may differ from a plain program's by a relative error of at most 0.008.
Values may be sent and summed in bfloat16 or wider, within the bound.
A program may use at most 128 MiB of HBM per device.

v0:
```python
import functools

import jax
import jax.numpy as jnp
from jax import lax
from jax.experimental import pallas as pl
from jax.experimental.pallas import tpu as pltpu
from jax.sharding import PartitionSpec as P

HEADS = 16
HEAD = 64
CORES = 2
LANES = 128

eps = 1e-06
LOW = -1e30
time_forms = ("sabhe,tabhe->abhst", "abhst,tabhe->sabhe")
height_forms = ("asbhe,atbhe->abhst", "abhst,atbhe->asbhe")


def attend_group(state, block, w_in, w_back, bias, normed, context):
    tokens, width = state.shape
    band = min(256, width)
    per_band = band // HEAD
    floats = state.astype(jnp.float32)
    power = jnp.mean(floats * floats, axis=-1, keepdims=True)
    normed[...] = (floats * lax.rsqrt(power + eps)).astype(jnp.bfloat16)
    lane_head = lax.broadcasted_iota(jnp.int32, (tokens, band), 1) // HEAD
    for start in range(0, width, band):
        pieces = [
            jnp.dot(
                normed[...],
                w_in[block, :, which * width + start : which * width + start + band],
                preferred_element_type=jnp.float32,
            ).astype(jnp.bfloat16)
            for which in range(3)
        ]
        query, keys, values = pieces
        alone = jnp.concatenate(
            [jnp.where(lane_head == head, query, jnp.zeros_like(query)) for head in range(per_band)], axis=0
        )
        scores = lax.dot_general(
            alone, keys, (((1,), (1,)), ((), ())), preferred_element_type=jnp.float32
        )
        expos, shares = [], []
        for head in range(per_band):
            block_scores = scores[head * tokens : (head + 1) * tokens] + bias[...]
            top = jnp.max(block_scores, axis=-1, keepdims=True)
            expo = jnp.exp((block_scores - top) * (1.0 / HEAD**0.5))
            shares.append(1.0 / jnp.sum(expo, axis=-1, keepdims=True))
            expos.append(expo.astype(jnp.bfloat16))
        parts = jnp.dot(jnp.concatenate(expos, axis=0), values, preferred_element_type=jnp.float32)
        mixed = parts[:tokens] * shares[0]
        for head in range(1, per_band):
            part = parts[head * tokens : (head + 1) * tokens] * shares[head]
            mixed = jnp.where(lane_head == head, part, mixed)
        context[:, start : start + band] = mixed.astype(jnp.bfloat16)
    update = jnp.dot(context[...], w_back[block], preferred_element_type=jnp.float32)
    return (state.astype(jnp.float32) + update).astype(jnp.bfloat16)


def line_bias(bias, line_of):
    shape = bias.shape
    first = line_of(lax.broadcasted_iota(jnp.int32, shape, 0))
    second = line_of(lax.broadcasted_iota(jnp.int32, shape, 1))
    bias[...] = jnp.where(first == second, 0.0, LOW).astype(jnp.float32)


def split_lanes(rows):
    return jnp.stack([rows[:, at : at + LANES] for at in range(0, rows.shape[1], LANES)])


def far_first(at, count):
    half = count // 2
    return half + at - at // half * (2 * at + half + 1 - count)


def column_kernel(
    mems, grps, frames, rows, steps,
    x_ref, w_in_hbm, w_back_hbm, out_ref,
    tokens_in, wide, apart, held, w_in, w_back, bias, normed, context,
    x_sem, w_sem, send_in, recv_in, send_out, recv_out,
):
    places = mems * grps
    small, width = held.shape[1], held.shape[2]
    per_step = mems // steps
    my_mem, my_grp = lax.axis_index("mem"), lax.axis_index("grp")
    me = my_mem * grps + my_grp
    my_pair, my_part = my_grp // CORES, my_mem // per_step

    arrive = pltpu.make_async_copy(x_ref, tokens_in, x_sem)
    arrive.start()
    weights = []
    for block in range(2):
        weights.append(pltpu.make_async_copy(w_in_hbm.at[block], w_in.at[block], w_sem.at[block, 0]))
        weights.append(pltpu.make_async_copy(w_back_hbm.at[block], w_back.at[block], w_sem.at[block, 1]))
    barrier = pltpu.get_barrier_semaphore()

    @pl.loop(1, places)
    def _(offset):
        other = (me + offset) % places
        pl.semaphore_signal(barrier, inc=1, device_id={"mem": other // grps, "grp": other % grps})

    arrive.wait()
    for copy in weights:
        copy.start()

    @pl.loop(0, small)
    def _(at):
        wide[:, pl.ds(pl.multiple_of(at * places, places), places), :] = split_lanes(
            tokens_in[at].astype(jnp.float32)
        )

    pl.semaphore_wait(barrier, places - 1)

    def inward(place):
        return pltpu.make_async_remote_copy(
            src_ref=apart.at[place],
            dst_ref=held.at[me],
            send_sem=send_in.at[place],
            recv_sem=recv_in.at[me],
            device_id={"mem": place // grps, "grp": place % grps},
        )

    @pl.loop(0, places)
    def _(at):
        core, rest = at // (places // CORES), at % (places // CORES)
        to_pair = (my_pair + rest // mems) % (grps // CORES)
        to_part = (my_part + far_first(rest % mems // per_step, steps)) % steps
        to_mem = to_part * per_step + (my_mem + rest) % per_step
        place = to_mem * grps + to_pair * CORES + core
        for lane in range(wide.shape[0]):
            column = wide[lane, pl.ds(place, small, stride=places), :]
            apart[place, :, lane * LANES : (lane + 1) * LANES] = column.astype(apart.dtype)

        @pl.when(place == me)
        def _():
            pltpu.make_async_copy(apart.at[me], held.at[me], recv_in.at[me]).start()

        @pl.when(place != me)
        def _():
            inward(place).start()

    line_bias(bias, lambda at: at % rows)
    weights[0].wait()
    weights[1].wait()

    @pl.loop(0, grps)
    def _(turn):
        pair = (my_pair + turn // CORES) % (grps // CORES)
        grp = pair * CORES + (my_grp + turn) % CORES

        @pl.loop(0, mems)
        def _(mem):
            place = mem * grps + grp
            pltpu.make_async_copy(apart.at[place], held.at[place], recv_in.at[place]).wait()

        state = jnp.concatenate([held[mem * grps + grp] for mem in range(mems)], axis=0)
        done = attend_group(state, 0, w_in, w_back, bias, normed, context)
        for mem in range(mems):
            held[mem * grps + grp] = done[mem * small : (mem + 1) * small]

    line_bias(bias, lambda at: at // (grps * small) * frames + at // rows % frames)
    weights[2].wait()
    weights[3].wait()

    def outward(place):
        return pltpu.make_async_remote_copy(
            src_ref=held.at[place],
            dst_ref=out_ref.at[me],
            send_sem=send_out.at[place],
            recv_sem=recv_out.at[me],
            device_id={"mem": place // grps, "grp": place % grps},
        )

    count = per_step * grps

    @pl.loop(0, steps)
    def _(turn):
        step = (my_part + far_first(turn, steps)) % steps
        first = step * count
        state = jnp.concatenate([held[first + at] for at in range(count)], axis=0)
        done = attend_group(state, 1, w_in, w_back, bias, normed, context)
        for at in range(count):
            held[first + at] = done[at * small : (at + 1) * small]

        @pl.loop(0, count)
        def _(at):
            place = first + at

            @pl.when(place == me)
            def _():
                pltpu.make_async_copy(held.at[me], out_ref.at[me], recv_out.at[me]).start()

            @pl.when(place != me)
            def _():
                outward(place).start()

    @pl.loop(1, places)
    def _(offset):
        place = (me + offset) % places
        inward(place).wait_send()
        outward(place).wait_send()

    @pl.loop(0, places)
    def _(place):
        pltpu.make_async_copy(held.at[place], out_ref.at[place], recv_out.at[place]).wait()


def by_column(mems, grps, video, w_triple, w_out):
    frames, rows, cols, width = video.shape
    places, small = mems * grps, frames * rows
    steps = 4 if mems % 4 == 0 else mems
    tokens = mems * small
    dma = pltpu.SemaphoreType.DMA
    back = pl.pallas_call(
        functools.partial(column_kernel, mems, grps, frames, rows, steps),
        out_shape=jax.ShapeDtypeStruct((places, small, width), video.dtype),
        in_specs=[pl.BlockSpec(memory_space=pl.ANY)] * 3,
        out_specs=pl.BlockSpec(memory_space=pl.ANY),
        scratch_shapes=[
            pltpu.VMEM((small, places, width), video.dtype),
            pltpu.VMEM((width // LANES, small * places, LANES), jnp.float32),
            pltpu.VMEM((places, small, width), video.dtype),
            pltpu.VMEM((places, small, width), video.dtype),
            pltpu.VMEM(w_triple.shape, w_triple.dtype),
            pltpu.VMEM(w_out.shape, w_out.dtype),
            pltpu.VMEM((tokens, tokens), jnp.float32),
            pltpu.VMEM((tokens, width), video.dtype),
            pltpu.VMEM((tokens, width), video.dtype),
            dma,
            dma((2, 2)),
            dma((places,)),
            dma((places,)),
            dma((places,)),
            dma((places,)),
        ],
        compiler_params=pltpu.CompilerParams(
            collective_id=0, has_side_effects=True, vmem_limit_bytes=60 * 2**20
        ),
    )(video.reshape(small, cols, width), w_triple, w_out)
    return jnp.transpose(back.reshape(cols, frames, rows, width), (1, 2, 0, 3))


def attend_local(triple, forms):
    lead = triple.shape[:-1]
    width = triple.shape[-1] // 3
    pieces = triple.reshape(lead + (3, HEADS, HEAD))
    query = pieces[..., 0, :, :]
    keys = pieces[..., 1, :, :]
    values = pieces[..., 2, :, :]
    scores = jnp.einsum(forms[0], query, keys, preferred_element_type=jnp.float32) * (
        1.0 / HEAD**0.5
    )
    top = jnp.max(scores, axis=-1, keepdims=True)
    expo = jnp.exp(scores - top)
    probs = (expo / jnp.sum(expo, axis=-1, keepdims=True)).astype(jnp.bfloat16)
    context = jnp.einsum(forms[1], probs, values, preferred_element_type=jnp.float32)
    return context.astype(jnp.bfloat16).reshape(lead + (width,))


def make_triple(state, weight_in):
    width = state.shape[-1]
    floats = state.astype(jnp.float32)
    normed = (floats * lax.rsqrt(jnp.mean(floats * floats, axis=-1, keepdims=True) + eps)).astype(
        jnp.bfloat16
    )
    triple = jnp.dot(normed.reshape(-1, width), weight_in, preferred_element_type=jnp.float32)
    return triple.astype(jnp.bfloat16).reshape(state.shape[:-1] + (3 * width,))


def add_update(state, context, weight_back):
    width = state.shape[-1]
    update = jnp.dot(context.reshape(-1, width), weight_back, preferred_element_type=jnp.float32)
    return (state.astype(jnp.float32) + update.reshape(state.shape)).astype(jnp.bfloat16)


def whole_block(state, weight_in, weight_back, forms):
    context = attend_local(make_triple(state, weight_in), forms)
    return add_update(state, context, weight_back)


def by_lines(video, w_triple, w_out):
    regrouped = whole_block(
        lax.all_to_all(video, "mem", split_axis=2, concat_axis=0, tiled=True),
        w_triple[0],
        w_out[0],
        time_forms,
    )
    height_done = whole_block(
        lax.all_to_all(regrouped, "grp", split_axis=0, concat_axis=1, tiled=True),
        w_triple[1],
        w_out[1],
        height_forms,
    )
    return lax.all_to_all(
        lax.all_to_all(height_done, "grp", split_axis=1, concat_axis=0, tiled=True),
        "mem",
        split_axis=0,
        concat_axis=2,
        tiled=True,
    )


def solution(mesh):
    mems, grps = mesh.shape["mem"], mesh.shape["grp"]

    def on_device(video, w_triple, w_out):
        if video.shape[2] == mems * grps and mems == 4 * (mems // 4) == (mems // 4) * grps and grps % CORES == 0:
            return by_column(mems, grps, video, w_triple, w_out)
        return by_lines(video, w_triple, w_out)

    return jax.shard_map(
        on_device,
        mesh=mesh,
        in_specs=(P("mem", "grp", None, None), P(), P()),
        out_specs=P("mem", "grp", None, None),
        check_vma=False,
    )
```

profile of v0, /device:TPU:15, one launch (start us, length us, event | category | flops | bytes accessed | tf_op | source)
XLA Modules:
  0.0 105.6 jit_solution(6717127678036768710)
XLA Ops:
  0.0 101.6 %shard_map.37 = bf16[32,32,1024]{2,1,0:T(8,128)(2,1)} custom-call(bf16[32,32,1024]{2,1,0:T(8,128)(2,1)} %bitcast.6, bf16[2,1024,3072]{2,1,0:T(8,128)(2,1)} %w_in_hbm.1, bf16[2,1024,1024]{2,1,0:T(8,128)(2,1)} %w_back_hbm.1), custom_call_target="tpu_custom_call" | custom-call | tf_op jit(solution)/shard_map/pallas_call | solution.py:216
  101.6 4.1 %copy.6 = bf16[32,4,8,1024]{3,0,2,1:T(8,128)(2,1)} copy(bf16[32,4,8,1024]{3,2,1,0:T(8,128)(2,1)} %bitcast.5) | data formatting | bytes 4194304 | tf_op jit(solution)/shard_map/reshape | solution.py:242
where the time goes:
time: 106 us
  Pallas kernels  102 us (96%)
  local copies, waits for them, and re-layouts  4.07 us (4%)
    pallas_call x1, Pallas kernels, by_column(): pl.pallas_call(functools.partial(column_kernel, mems, grps, frames, rows,...  102 us
    reshape x1, local copies, waits for them, and re-layouts, by_column(): return jnp.transpose(back.reshape(cols, frames, rows, width), (1, 2, 0, 3))  4.07 us

commit v1 on v0

--- a/solution.py
+++ b/solution.py
@@ -13,7 +13,7 @@
 LANES = 128
 
 eps = 1e-06
-LOW = -1e30
+MASKED = -1e30
 time_forms = ("sabhe,tabhe->abhst", "abhst,tabhe->sabhe")
 height_forms = ("asbhe,atbhe->abhst", "abhst,atbhe->asbhe")
 
@@ -63,23 +63,45 @@
     shape = bias.shape
     first = line_of(lax.broadcasted_iota(jnp.int32, shape, 0))
     second = line_of(lax.broadcasted_iota(jnp.int32, shape, 1))
-    bias[...] = jnp.where(first == second, 0.0, LOW).astype(jnp.float32)
+    bias[...] = jnp.where(first == second, 0.0, MASKED).astype(jnp.float32)
 
 
 def split_lanes(rows):
     return jnp.stack([rows[:, at : at + LANES] for at in range(0, rows.shape[1], LANES)])
 
 
-def far_first(at, count):
-    half = count // 2
-    return half + at - at // half * (2 * at + half + 1 - count)
+LEVELS = 4
+SAME, HALF, LOWER, UPPER = 0, 1, 2, 3
+INNER_ORDER = (
+    (LOWER, 0, 0), (UPPER, 0, 0), (LOWER, 0, 1), (UPPER, 0, 1), (HALF, 0, 0), (SAME, 0, 0), (HALF, 0, 1), (SAME, 0, 1),
+    (LOWER, 1, 0), (UPPER, 1, 0), (LOWER, 1, 1), (UPPER, 1, 1), (HALF, 1, 0), (SAME, 1, 0), (HALF, 1, 1), (SAME, 1, 1),
+)
+OUTER_ORDER = (
+    (HALF, 0, 0), (HALF, 0, 1), (HALF, 1, 0), (HALF, 1, 1), (LOWER, 0, 0), (UPPER, 0, 0), (SAME, 0, 0), (LOWER, 0, 1),
+    (UPPER, 0, 1), (SAME, 0, 1), (SAME, 1, 0), (SAME, 1, 1), (LOWER, 1, 0), (UPPER, 1, 0), (LOWER, 1, 1), (UPPER, 1, 1),
+)
+HELD = 4
+HELD_TURNS = 2
+
+
+def looked_up(at, table):
+    found = table[0]
+    for index in range(1, len(table)):
+        found = jnp.where(at == index, table[index], found)
+    return found
+
+
+def level_of(kind, level):
+    near = level + kind - 2 * kind * (level % 2)
+    far = (1 - level // 2) * 2 + kind - LOWER
+    return jnp.where(kind < LOWER, near, far)
 
 
 def column_kernel(
     mems, grps, frames, rows, steps,
     x_ref, w_in_hbm, w_back_hbm, out_ref,
     tokens_in, wide, apart, held, w_in, w_back, bias, normed, context,
-    x_sem, w_sem, send_in, recv_in, send_out, recv_out,
+    x_sem, w_sem, send_in, recv_in, send_out, recv_out, go,
 ):
     places = mems * grps
     small, width = held.shape[1], held.shape[2]
@@ -87,6 +109,7 @@
     my_mem, my_grp = lax.axis_index("mem"), lax.axis_index("grp")
     me = my_mem * grps + my_grp
     my_pair, my_part = my_grp // CORES, my_mem // per_step
+    outer = (my_part + my_part // 2) % 2 == 0
 
     arrive = pltpu.make_async_copy(x_ref, tokens_in, x_sem)
     arrive.start()
@@ -122,13 +145,27 @@
             device_id={"mem": place // grps, "grp": place % grps},
         )
 
+    def place_of(at):
+        turn = at // per_step
+        kind, core, pair = (
+            jnp.where(outer, looked_up(turn, [a[k] for a in OUTER_ORDER]), looked_up(turn, [a[k] for a in INNER_ORDER]))
+            for k in range(3)
+        )
+        to_pair = (my_pair + pair) % (grps // CORES)
+        to_mem = level_of(kind, my_part) * per_step + (my_mem + at) % per_step
+        return to_mem * grps + to_pair * CORES + core
+
+    held_back = places - places // HELD
+    my_core = my_grp % CORES
+
+    def start_held():
+        @pl.loop(held_back, places)
+        def _(at):
+            inward(place_of(at)).start()
+
     @pl.loop(0, places)
     def _(at):
-        core, rest = at // (places // CORES), at % (places // CORES)
-        to_pair = (my_pair + rest // mems) % (grps // CORES)
-        to_part = (my_part + far_first(rest % mems // per_step, steps)) % steps
-        to_mem = to_part * per_step + (my_mem + rest) % per_step
-        place = to_mem * grps + to_pair * CORES + core
+        place = place_of(at)
         for lane in range(wide.shape[0]):
             column = wide[lane, pl.ds(place, small, stride=places), :]
             apart[place, :, lane * LANES : (lane + 1) * LANES] = column.astype(apart.dtype)
@@ -137,9 +174,14 @@
         def _():
             pltpu.make_async_copy(apart.at[me], held.at[me], recv_in.at[me]).start()
 
-        @pl.when(place != me)
+        @pl.when((place != me) & ~(outer & (at >= held_back)))
         def _():
             inward(place).start()
+
+    @pl.when(outer & (my_core == 1))
+    def _():
+        pl.semaphore_wait(go, 1)
+        start_held()
 
     line_bias(bias, lambda at: at % rows)
     weights[0].wait()
@@ -159,6 +201,11 @@
         done = attend_group(state, 0, w_in, w_back, bias, normed, context)
         for mem in range(mems):
             held[mem * grps + grp] = done[mem * small : (mem + 1) * small]
+
+        @pl.when(outer & (my_core == 0) & (turn == HELD_TURNS - 1))
+        def _():
+            pl.semaphore_signal(go, inc=1, device_id={"mem": my_mem, "grp": my_grp + 1})
+            start_held()
 
     line_bias(bias, lambda at: at // (grps * small) * frames + at // rows % frames)
     weights[2].wait()
@@ -177,7 +224,11 @@
 
     @pl.loop(0, steps)
     def _(turn):
-        step = (my_part + far_first(turn, steps)) % steps
+        late = outer & (my_core == 0)
+        kind = jnp.where(
+            late, looked_up(turn, [HALF, LOWER, UPPER, SAME]), looked_up(turn, [LOWER, UPPER, HALF, SAME])
+        )
+        step = level_of(kind, my_part)
         first = step * count
         state = jnp.concatenate([held[first + at] for at in range(count)], axis=0)
         done = attend_group(state, 1, w_in, w_back, bias, normed, context)
@@ -186,7 +237,9 @@
 
         @pl.loop(0, count)
         def _(at):
-            place = first + at
+            to_mem = (my_mem + at // grps) % per_step
+            to_pair = (my_pair + at % grps // CORES) % (grps // CORES)
+            place = first + to_mem * grps + to_pair * CORES + (my_core + at) % CORES
 
             @pl.when(place == me)
             def _():
@@ -210,7 +263,7 @@
 def by_column(mems, grps, video, w_triple, w_out):
     frames, rows, cols, width = video.shape
     places, small = mems * grps, frames * rows
-    steps = 4 if mems % 4 == 0 else mems
+    steps = LEVELS
     tokens = mems * small
     dma = pltpu.SemaphoreType.DMA
     back = pl.pallas_call(
@@ -234,6 +287,7 @@
             dma((places,)),
             dma((places,)),
             dma((places,)),
+            pltpu.SemaphoreType.REGULAR,
         ],
         compiler_params=pltpu.CompilerParams(
             collective_id=0, has_side_effects=True, vmem_limit_bytes=60 * 2**20

time: 106 us -> 104 us (0.981)
  the two profiles are of different devices: /device:TPU:15 before, /device:TPU:12 now
where the time goes in v1:
time: 104 us; the launch traced here: 103 us
  Pallas kernels  99.3 us (95%)
  local copies, waits for them, and re-layouts  4.07 us (4%)
    pallas_call x1, Pallas kernels, by_column(): pl.pallas_call(functools.partial(column_kernel, mems, grps, frames, rows,...  99.3 us
    reshape x1, local copies, waits for them, and re-layouts, by_column(): return jnp.transpose(back.reshape(cols, frames, rows, width), (1, 2, 0, 3))  4.07 us

profile of v1, /device:TPU:12, one launch (start us, length us, event | category | flops | bytes accessed | tf_op | source)
XLA Modules:
  0.0 103.4 jit_solution(6858832565269169121)
XLA Ops:
  0.0 99.3 %shard_map.37 = bf16[32,32,1024]{2,1,0:T(8,128)(2,1)} custom-call(bf16[32,32,1024]{2,1,0:T(8,128)(2,1)} %bitcast.6, bf16[2,1024,3072]{2,1,0:T(8,128)(2,1)} %w_in_hbm.1, bf16[2,1024,1024]{2,1,0:T(8,128)(2,1)} %w_back_hbm.1), custom_call_target="tpu_custom_call" | custom-call | tf_op jit(solution)/shard_map/pallas_call | solution.py:269
  99.4 4.1 %copy.6 = bf16[32,4,8,1024]{3,0,2,1:T(8,128)(2,1)} copy(bf16[32,4,8,1024]{3,2,1,0:T(8,128)(2,1)} %bitcast.5) | data formatting | bytes 4194304 | tf_op jit(solution)/shard_map/reshape | solution.py:296

commit v2 on v1

--- a/solution.py
+++ b/solution.py
@@ -290,7 +290,7 @@
             pltpu.SemaphoreType.REGULAR,
         ],
         compiler_params=pltpu.CompilerParams(
-            collective_id=0, has_side_effects=True, vmem_limit_bytes=60 * 2**20
+            collective_id=0, has_side_effects=True, vmem_limit_bytes=50 * 2**20
         ),
     )(video.reshape(small, cols, width), w_triple, w_out)
     return jnp.transpose(back.reshape(cols, frames, rows, width), (1, 2, 0, 3))

time: 104 us -> 102 us (0.981)
  local copies, waits for them, and re-layouts: 4.07 us -> 2.47 us
    reshape x1, local copies, waits for them, and re-layouts: 4.07 us -> 2.47 us  [by_column(): return jnp.transpose(back.reshape(cols, frames, rows, width), (1, 2, 0, 3))]
where the time goes in v2:
time: 102 us
  Pallas kernels  99.1 us (97%)
  local copies, waits for them, and re-layouts  2.47 us (2%)
    pallas_call x1, Pallas kernels, by_column(): pl.pallas_call(functools.partial(column_kernel, mems, grps, frames, rows,...  99.1 us
    reshape x1, local copies, waits for them, and re-layouts, by_column(): return jnp.transpose(back.reshape(cols, frames, rows, width), (1, 2, 0, 3))  2.47 us

profile of v2, /device:TPU:12, one launch (start us, length us, event | category | flops | bytes accessed | tf_op | source)
XLA Modules:
  0.0 101.6 jit_solution(18168385849966332428)
XLA Ops:
  0.0 99.1 %shard_map.37 = bf16[32,32,1024]{2,1,0:T(8,128)(2,1)S(1)} custom-call(bf16[32,32,1024]{2,1,0:T(8,128)(2,1)} %bitcast.6, bf16[2,1024,3072]{2,1,0:T(8,128)(2,1)} %w_in_hbm.1, bf16[2,1024,1024]{2,1,0:T(8,128)(2,1)} %w_back_hbm.1), custom_call_target="tpu_custom_call" | custom-call | tf_op jit(solution)/shard_map/pallas_call | solution.py:269
  99.1 2.5 %copy.6 = bf16[32,4,8,1024]{3,0,2,1:T(8,128)(2,1)} copy(bf16[32,4,8,1024]{3,2,1,0:T(8,128)(2,1)S(1)} %bitcast.5) | data formatting | bytes 4194304 | tf_op jit(solution)/shard_map/reshape | solution.py:296

commit v3 on v2

--- a/solution.py
+++ b/solution.py
@@ -237,9 +237,9 @@
 
         @pl.loop(0, count)
         def _(at):
-            to_mem = (my_mem + at // grps) % per_step
-            to_pair = (my_pair + at % grps // CORES) % (grps // CORES)
-            place = first + to_mem * grps + to_pair * CORES + (my_core + at) % CORES
+            to_mem = (my_mem + at) % per_step
+            to_pair = (my_pair + at // per_step) % (grps // CORES)
+            place = first + to_mem * grps + to_pair * CORES + (my_core + at // grps) % CORES
 
             @pl.when(place == me)
             def _():

time: 102 us -> 101 us (level)
  no operation moved by 1% of the time
where the time goes in v3:
time: 101 us
  Pallas kernels  98.2 us (97%)
  local copies, waits for them, and re-layouts  2.47 us (2%)
    pallas_call x1, Pallas kernels, by_column(): pl.pallas_call(functools.partial(column_kernel, mems, grps, frames, rows,...  98.2 us
    reshape x1, local copies, waits for them, and re-layouts, by_column(): return jnp.transpose(back.reshape(cols, frames, rows, width), (1, 2, 0, 3))  2.47 us

profile of v3, /device:TPU:12, one launch (start us, length us, event | category | flops | bytes accessed | tf_op | source)
XLA Modules:
  0.0 100.7 jit_solution(14419549411900501293)
XLA Ops:
  0.0 98.2 %shard_map.37 = bf16[32,32,1024]{2,1,0:T(8,128)(2,1)S(1)} custom-call(bf16[32,32,1024]{2,1,0:T(8,128)(2,1)} %bitcast.6, bf16[2,1024,3072]{2,1,0:T(8,128)(2,1)} %w_in_hbm.1, bf16[2,1024,1024]{2,1,0:T(8,128)(2,1)} %w_back_hbm.1), custom_call_target="tpu_custom_call" | custom-call | tf_op jit(solution)/shard_map/pallas_call | solution.py:269
  98.2 2.5 %copy.6 = bf16[32,4,8,1024]{3,0,2,1:T(8,128)(2,1)} copy(bf16[32,4,8,1024]{3,2,1,0:T(8,128)(2,1)S(1)} %bitcast.5) | data formatting | bytes 4194304 | tf_op jit(solution)/shard_map/reshape | solution.py:296

commit v4 on v3

--- a/solution.py
+++ b/solution.py
@@ -81,7 +81,7 @@
     (UPPER, 0, 1), (SAME, 0, 1), (SAME, 1, 0), (SAME, 1, 1), (LOWER, 1, 0), (UPPER, 1, 0), (LOWER, 1, 1), (UPPER, 1, 1),
 )
 HELD = 4
-HELD_TURNS = 2
+HELD_TURNS = 1
 
 
 def looked_up(at, table):

time: 101 us -> 100 us (0.990)
  no operation moved by 1% of the time
where the time goes in v4:
time: 100 us
  Pallas kernels  97.7 us (98%)
  local copies, waits for them, and re-layouts  2.47 us (2%)
    pallas_call x1, Pallas kernels, by_column(): pl.pallas_call(functools.partial(column_kernel, mems, grps, frames, rows,...  97.7 us
    reshape x1, local copies, waits for them, and re-layouts, by_column(): return jnp.transpose(back.reshape(cols, frames, rows, width), (1, 2, 0, 3))  2.47 us

profile of v4, /device:TPU:12, one launch (start us, length us, event | category | flops | bytes accessed | tf_op | source)
XLA Modules:
  0.0 100.2 jit_solution(436160816448679085)
XLA Ops:
  0.0 97.7 %shard_map.37 = bf16[32,32,1024]{2,1,0:T(8,128)(2,1)S(1)} custom-call(bf16[32,32,1024]{2,1,0:T(8,128)(2,1)} %bitcast.6, bf16[2,1024,3072]{2,1,0:T(8,128)(2,1)} %w_in_hbm.1, bf16[2,1024,1024]{2,1,0:T(8,128)(2,1)} %w_back_hbm.1), custom_call_target="tpu_custom_call" | custom-call | tf_op jit(solution)/shard_map/pallas_call | solution.py:269
  97.7 2.5 %copy.6 = bf16[32,4,8,1024]{3,0,2,1:T(8,128)(2,1)} copy(bf16[32,4,8,1024]{3,2,1,0:T(8,128)(2,1)S(1)} %bitcast.5) | data formatting | bytes 4194304 | tf_op jit(solution)/shard_map/reshape | solution.py:296
